TPU v7x, 512 devices: a whole 4x8x8 slice. The times are simulated.
512 devices in a mesh: space: 64 (over y, z), orb: 8 (over x, core).
Axes of the slice: x: 4, y: 8, z: 8, core: 2. Of those that a mesh axis runs over, the one named last changes fastest.
Arguments:
- hamiltonian: bfloat16 [512, 7, 256, 256], P('space'), may hold values from -0.125 to 0.125
- orbitals: bfloat16 [256, 131072], P('orb', 'space'), may hold values from -6 to 6
- adjacency: int32 [512, 6], P('space'), may hold values from 0 to 511, as said below
Outputs:
- basis: float32 [256, 131072], P('orb', 'space')
- factor: float32 [256, 256], replicated
Inputs may be any that keep to these rules, and one draw needn't show every extreme that they name: `adjacency`: with elements in blocks of 8 (block b holds elements b * 8 to b * 8 + 7), face 0 of an element in block b lies in block b - 1 and face 1 in block b + 1 (both modulo the number of blocks), faces 2 to 5 in block b; for each face, the elements of a block name every element of the target block exactly once.
All inputs are finite; a program needn't handle non-finite values.
Results may differ from a plain program's by a relative error of at most 0.0041.
Values may be sent and summed in bfloat16 or wider, within the bound.
A program may use at most 64 MiB of HBM per device.

v0:
```python
import jax
import jax.numpy as jnp
from jax import lax
from jax.sharding import PartitionSpec as P

centre = 0.25
radius = 0.75


def with_halo(block, sides, width):
    for axis, dim in sides:
        count = lax.axis_size(axis)
        forward = [(i, i + 1) for i in range(count - 1)]
        forward.append((count - 1, 0))
        backward = [(target, source) for source, target in forward]
        low = lax.ppermute(
            lax.slice_in_dim(block, block.shape[dim] - width, None, axis=dim), axis, forward
        )
        high = lax.ppermute(lax.slice_in_dim(block, 0, width, axis=dim), axis, backward)
        block = jnp.concatenate([low, block, high], axis=dim)
    return block


def shards(hamiltonian, orbitals, adjacency):
    count = hamiltonian.shape[0]
    width = hamiltonian.shape[2]
    owned = orbitals.shape[0]
    total = count * lax.axis_size("space")
    first = lax.axis_index("space") * count
    located = (adjacency - first + count) % total

    def apply_ham(vec):
        padded = with_halo(vec, (("space", 1),), count * width)
        blocks = padded.reshape(owned, 3 * count, width)
        near = jnp.take(blocks, located.reshape(-1), axis=1).reshape(owned, count, 6, width)
        own_part = vec.reshape(owned, count, width)
        result = jnp.einsum(
            "oej,eij->oei", own_part, hamiltonian[:, 0], preferred_element_type=jnp.float32
        )
        result = result + jnp.einsum(
            "oefj,efij->oei", near, hamiltonian[:, 1:], preferred_element_type=jnp.float32
        )
        return result.reshape(owned, count * width)

    level_zero = orbitals.astype(jnp.float32)
    level_one = ((apply_ham(orbitals) - centre * level_zero) / radius).astype(jnp.bfloat16)
    one_wide = level_one.astype(jnp.float32)
    level_two = (2.0 * (apply_ham(level_one) - centre * one_wide) / radius - level_zero).astype(
        jnp.bfloat16
    )
    two_wide = level_two.astype(jnp.float32)
    filtered = 2.0 * (apply_ham(level_two) - centre * two_wide) / radius - one_wide
    row_piece = lax.all_to_all(filtered, "orb", split_axis=1, concat_axis=0, tiled=True)
    partial_gram = jnp.dot(row_piece, row_piece.T, precision=lax.Precision.HIGHEST)
    gram = lax.psum(partial_gram, ("space", "orb"))
    lower = jnp.linalg.cholesky(gram)
    solved = lax.linalg.triangular_solve(lower, row_piece, left_side=True, lower=True)
    basis = lax.all_to_all(solved, "orb", split_axis=0, concat_axis=1, tiled=True)
    return (basis, lower.T)


def solution(mesh):
    in_specs = (P("space", None, None, None), P("orb", "space"), P("space", None))
    out_specs = (P("orb", "space"), P())
    return jax.shard_map(shards, mesh=mesh, in_specs=in_specs, out_specs=out_specs, check_vma=False)
```

profile of v0, /device:TPU:1, one launch (start us, length us, event | category | flops | bytes accessed | tf_op | source)
XLA Modules:
  0.0 434.9 jit_solution(6208198198700955853)
XLA Ops:
  7.2 0.0 copy-start
  7.2 5.0 %collective-permute-start = (bf16[32,2048]{1,0:T(8,128)(2,1)}, bf16[32,2048]{1,0:T(8,128)(2,1)S(1)}, u32[]{:S(2)}, u32[]{:S(2)}) collective-permute-start(bf16[32,2048]{1,0:T(8,128)(2,1)} %param.6), channel_id=1, source_target_pairs={{0,8},{8,16},{16,24},{24,32},{32,40},{40,48},{48,56},{56,64},{64,7... | collective-permute-start | bytes 393224 | tf_op jit(solution)/shard_map/ppermute | solution.py:16
  12.1 11.5 %collective-permute-start.1 = (bf16[32,2048]{1,0:T(8,128)(2,1)}, bf16[32,2048]{1,0:T(8,128)(2,1)S(1)}, u32[]{:S(2)}, u32[]{:S(2)}) collective-permute-start(bf16[32,2048]{1,0:T(8,128)(2,1)} %param.6), channel_id=1, source_target_pairs={{8,0},{16,8},{24,16},{32,24},{40,32},{48,40},{56,48},{64,56},{72,6... | collective-permute-start | bytes 393224 | tf_op jit(solution)/shard_map/ppermute | solution.py:19
  23.6 0.7 add_select_fusion
  24.3 0.1 reshape.77
  24.5 0.6 collective-permute-done
  25.1 1.0 collective-permute-done.1
  26.1 0.9 pad_maximum_fusion
  27.1 0.6 gather_fusion
  27.7 0.1 broadcast_select_fusion.2
  27.9 4.7 %fusion.6 = f32[32,8,256]{2,0,1:T(8,128)S(1)} fusion(bf16[32,8,6,256]{3,0,2,1:T(8,128)(2,1)S(1)} %bitcast.139, bf16[8,7,256,256]{3,2,1,0:T(8,128)(2,1)} %param.5), kind=kOutput, calls=%fused_computation.11 | convolution fusion | flops 201326592 | bytes 7340032 | tf_op jit(solution)/shard_map/oefj,efij->oei/dot_general | solution.py:40
  32.6 0.0 copy-done
  32.6 1.6 fusion.16
  34.3 1.9 collective-permute-start.2
  36.3 7.3 %collective-permute-start.3 = (bf16[32,2048]{1,0:T(8,128)(2,1)S(1)}, bf16[32,2048]{1,0:T(8,128)(2,1)S(1)}, u32[]{:S(2)}, u32[]{:S(2)}) collective-permute-start(bf16[32,2048]{1,0:T(8,128)(2,1)S(1)} %fusion.27), channel_id=1, source_target_pairs={{8,0},{16,8},{24,16},{32,24},{40,32},{48,40},{56,48},{64,56},{72,6... | collective-permute-start | bytes 393224 | tf_op jit(solution)/shard_map/ppermute | solution.py:19
  43.6 0.4 collective-permute-done.2
  44.0 1.5 collective-permute-done.3
  45.6 0.6 gather_fusion.1
  46.2 0.1 broadcast_select_fusion.1
  46.4 4.7 %fusion.9 = f32[8,32,256]{2,1,0:T(8,128)S(1)} fusion(bf16[32,8,6,256]{3,0,2,1:T(8,128)(2,1)S(1)} %bitcast.140, bf16[8,7,256,256]{3,2,1,0:T(8,128)(2,1)} %param.5), kind=kOutput, calls=%fused_computation.12 | convolution fusion | flops 201326592 | bytes 7340032 | tf_op jit(solution)/shard_map/oefj,efij->oei/dot_general | solution.py:40
  51.1 1.7 fusion.18
  52.8 0.1 fusion.28
  52.8 1.9 collective-permute-start.4
  54.8 7.1 %collective-permute-start.5 = (bf16[32,2048]{1,0:T(8,128)(2,1)S(1)}, bf16[32,2048]{1,0:T(8,128)(2,1)S(1)}, u32[]{:S(2)}, u32[]{:S(2)}) collective-permute-start(bf16[32,2048]{1,0:T(8,128)(2,1)S(1)} %fusion.28), channel_id=1, source_target_pairs={{8,0},{16,8},{24,16},{32,24},{40,32},{48,40},{56,48},{64,56},{72,6... | collective-permute-start | bytes 393224 | tf_op jit(solution)/shard_map/ppermute | solution.py:19
  61.9 0.4 collective-permute-done.4
  62.3 1.5 collective-permute-done.5
  63.9 0.6 gather_fusion.2
  64.5 0.1 broadcast_select_fusion
  64.6 4.7 %fusion.12 = f32[8,32,256]{2,1,0:T(8,128)S(1)} fusion(bf16[32,8,6,256]{3,0,2,1:T(8,128)(2,1)S(1)} %bitcast.138, bf16[8,7,256,256]{3,2,1,0:T(8,128)(2,1)} %param.5), kind=kOutput, calls=%fused_computation.13 | convolution fusion | flops 201326592 | bytes 7340032 | tf_op jit(solution)/shard_map/oefj,efij->oei/dot_general | solution.py:40
  69.4 1.7 fusion.17
  71.0 0.1 convert_subtract_fusion
  71.1 0.7 copy.78
  71.8 7.8 %all-to-all-start = ((f32[32,8,256]{2,0,1:T(8,128)}), f32[32,8,256]{2,0,1:T(8,128)S(1)}, u32[]{:S(2)}, u32[]{:S(2)}) async-start(f32[32,8,256]{2,0,1:T(8,128)} %bitcast.115), calls=%async_computation | async-start | bytes 524288 | tf_op jit(solution)/shard_map/all_to_all | solution.py:53
  79.7 0.0 all-reduce.3.cloned.1.call-start
  79.7 6.5 %all-to-all-done = f32[32,8,256]{2,0,1:T(8,128)S(1)} async-done(((f32[32,8,256]{2,0,1:T(8,128)}), f32[32,8,256]{2,0,1:T(8,128)S(1)}, u32[]{:S(2)}, u32[]{:S(2)}) %all-to-all-start) | async-done | bytes 262176 | tf_op jit(solution)/shard_map/all_to_all | solution.py:53
  86.1 1.1 fusion.49
  87.2 0.0 all-reduce.3.cloned.1.call-update
  87.3 266.3 %all-reduce.3.cloned.1.call-done = f32[256,256]{0,1:T(8,128)} async-done(((f32[256,256]{0,1:T(8,128)}), f32[256,256]{0,1:T(8,128)}) %all-reduce.3.cloned.1.call-update) | async-done | bytes 262160 | tf_op jit(solution)/shard_map/psum | solution.py:55
  353.6 1.1 copy.40
  354.7 1.0 fusion.31
  355.7 11.7 %cholesky.50 = f32[128,128]{1,0:T(8,128)S(1)} custom-call(f32[128,128]{1,0:T(8,128)S(1)} %cholesky.118), custom_call_target="Cholesky" | custom-call | tf_op jit(solution)/shard_map/jit(cholesky)/cholesky | solution.py:56
  367.5 9.8 %custom-call.14 = f32[1,128,128]{1,2,0:T(8,128)S(1)} custom-call(f32[1,128,128]{2,1,0:T(8,128)S(1)} %get-tuple-element.34), custom_call_target="InvertDiagBlocksLowerTriangular" | custom-call | tf_op jit(solution)/shard_map/jit(cholesky)/cholesky | solution.py:56
  377.3 0.2 constant_dynamic-update-slice_fusion.1
  377.5 0.3 convolution_subtract_fusion.1
  377.8 11.7 %cholesky.105 = f32[128,128]{1,0:T(8,128)S(1)} custom-call(f32[128,128]{1,0:T(8,128)S(1)} %convolution_subtract_fusion.1), custom_call_target="Cholesky" | custom-call | tf_op jit(solution)/shard_map/jit(cholesky)/cholesky | solution.py:56
  389.5 0.6 compare_reduce_fusion
  391.4 0.1 triangular_solve.61
  391.5 4.0 while.1
  391.7 0.6 fusion.61
  392.3 1.3 bitcast_dynamic-update-slice_fusion.2
  393.6 0.6 fusion.61
  394.2 1.3 bitcast_dynamic-update-slice_fusion.2
  395.5 19.7 %custom-call.15 = f32[2,128,128]{1,2,0:T(8,128)S(1)} custom-call(f32[2,128,128]{2,1,0:T(8,128)S(1)} %get-tuple-element.10), custom_call_target="InvertDiagBlocksLowerTriangular" | custom-call | tf_op jit(solution)/shard_map/triangular_solve | solution.py:57
  415.2 0.3 fusion.42
  415.5 0.3 convolution_subtract_fusion
  415.8 0.3 fusion.41
  416.1 0.7 pad_maximum_fusion.3
  416.8 4.0 all-to-all-start.1
  420.8 0.8 copy.42
  421.7 5.6 %all-to-all-done.1 = f32[8,32,256]{2,1,0:T(8,128)S(1)} async-done(((f32[8,32,256]{2,1,0:T(8,128)}), f32[8,32,256]{2,1,0:T(8,128)S(1)}, u32[]{:S(2)}, u32[]{:S(2)}) %all-to-all-start.1) | async-done | bytes 262176 | tf_op jit(solution)/shard_map/all_to_all | solution.py:58
  427.3 0.7 copy.58
  (22 shorter events, 0.5 us)
Async XLA Ops:
  7.2 25.4 %copy-start = (bf16[32,2048]{1,0:T(8,128)(2,1)S(1)}, bf16[32,2048]{1,0:T(8,128)(2,1)}, u32[]{:S(2)}) copy-start(bf16[32,2048]{1,0:T(8,128)(2,1)} %param.6) | copy-start | bytes 393220
  7.2 17.9 %collective-permute-start = (bf16[32,2048]{1,0:T(8,128)(2,1)}, bf16[32,2048]{1,0:T(8,128)(2,1)S(1)}, u32[]{:S(2)}, u32[]{:S(2)}) collective-permute-start(bf16[32,2048]{1,0:T(8,128)(2,1)} %param.6), channel_id=1, source_target_pairs={{0,8},{8,16},{16,24},{24,32},{32,40},{40,48},{48,56},{56,64},{64,7... | collective-permute-start | bytes 393224 | tf_op jit(solution)/shard_map/ppermute | solution.py:16
  12.1 14.0 %collective-permute-start.1 = (bf16[32,2048]{1,0:T(8,128)(2,1)}, bf16[32,2048]{1,0:T(8,128)(2,1)S(1)}, u32[]{:S(2)}, u32[]{:S(2)}) collective-permute-start(bf16[32,2048]{1,0:T(8,128)(2,1)} %param.6), channel_id=1, source_target_pairs={{8,0},{16,8},{24,16},{32,24},{40,32},{48,40},{56,48},{64,56},{72,6... | collective-permute-start | bytes 393224 | tf_op jit(solution)/shard_map/ppermute | solution.py:19
  34.3 9.7 %collective-permute-start.2 = (bf16[32,2048]{1,0:T(8,128)(2,1)S(1)}, bf16[32,2048]{1,0:T(8,128)(2,1)S(1)}, u32[]{:S(2)}, u32[]{:S(2)}) collective-permute-start(bf16[32,2048]{1,0:T(8,128)(2,1)S(1)} %fusion.27), channel_id=1, source_target_pairs={{0,8},{8,16},{16,24},{24,32},{32,40},{40,48},{48,56},{56,64},{64,7... | collective-permute-start | bytes 393224 | tf_op jit(solution)/shard_map/ppermute | solution.py:16
  36.3 9.3 %collective-permute-start.3 = (bf16[32,2048]{1,0:T(8,128)(2,1)S(1)}, bf16[32,2048]{1,0:T(8,128)(2,1)S(1)}, u32[]{:S(2)}, u32[]{:S(2)}) collective-permute-start(bf16[32,2048]{1,0:T(8,128)(2,1)S(1)} %fusion.27), channel_id=1, source_target_pairs={{8,0},{16,8},{24,16},{32,24},{40,32},{48,40},{56,48},{64,56},{72,6... | collective-permute-start | bytes 393224 | tf_op jit(solution)/shard_map/ppermute | solution.py:19
  52.8 9.4 %collective-permute-start.4 = (bf16[32,2048]{1,0:T(8,128)(2,1)S(1)}, bf16[32,2048]{1,0:T(8,128)(2,1)S(1)}, u32[]{:S(2)}, u32[]{:S(2)}) collective-permute-start(bf16[32,2048]{1,0:T(8,128)(2,1)S(1)} %fusion.28), channel_id=1, source_target_pairs={{0,8},{8,16},{16,24},{24,32},{32,40},{40,48},{48,56},{56,64},{64,7... | collective-permute-start | bytes 393224 | tf_op jit(solution)/shard_map/ppermute | solution.py:16
  54.8 9.0 %collective-permute-start.5 = (bf16[32,2048]{1,0:T(8,128)(2,1)S(1)}, bf16[32,2048]{1,0:T(8,128)(2,1)S(1)}, u32[]{:S(2)}, u32[]{:S(2)}) collective-permute-start(bf16[32,2048]{1,0:T(8,128)(2,1)S(1)} %fusion.28), channel_id=1, source_target_pairs={{8,0},{16,8},{24,16},{32,24},{40,32},{48,40},{56,48},{64,56},{72,6... | collective-permute-start | bytes 393224 | tf_op jit(solution)/shard_map/ppermute | solution.py:19
  71.8 14.3 %all-to-all-start = ((f32[32,8,256]{2,0,1:T(8,128)}), f32[32,8,256]{2,0,1:T(8,128)S(1)}, u32[]{:S(2)}, u32[]{:S(2)}) async-start(f32[32,8,256]{2,0,1:T(8,128)} %bitcast.115), calls=%async_computation | async-start | bytes 524288 | tf_op jit(solution)/shard_map/all_to_all | solution.py:53
  79.7 274.0 %all-reduce.3.cloned.1.call-start = ((), (), s32[]{:S(2)}) async-start(), calls=%async_computation.2 | async-start | bytes 524288 | tf_op jit(solution)/shard_map/psum | solution.py:55
  416.8 10.5 %all-to-all-start.1 = ((f32[8,32,256]{2,1,0:T(8,128)}), f32[8,32,256]{2,1,0:T(8,128)S(1)}, u32[]{:S(2)}, u32[]{:S(2)}) async-start(f32[8,32,256]{2,1,0:T(8,128)} %bitcast.26), calls=%async_computation.1 | async-start | bytes 524288 | tf_op jit(solution)/shard_map/all_to_all | solution.py:58
Sparse Core Ops, SparseCore 0:
  87.4 266.1 all-reduce.2
where the time goes:
time: 436 us; the launch traced here: 435 us
  waiting for transfers between devices  284 us (65%)
  other arithmetic  57.7 us (13%)
  starting transfers between devices  46.6 us (11%)
  matrix products  21.5 us (5%)
  between operations  15.5 us (4%)
  local copies, waits for them, and re-layouts  9.42 us (2%)
    psum x1, waiting for transfers between devices, shards(): gram = lax.psum(partial_gram, ('space', 'orb'))  266 us
    another operation x6, other arithmetic, shards(): lower = jnp.linalg.cholesky(gram)  33.9 us
    ppermute x3, starting transfers between devices, with_halo(): lax.ppermute(lax.slice_in_dim(block, 0, width, axis=dim), axis, backward)  25.9 us
    another operation x3, other arithmetic, shards(): lax.linalg.triangular_solve(lower, row_piece, left_side=True, lower=True)  20.4 us
    dot_general x3, matrix products, apply_ham(): jnp.einsum('oefj,efij->oei', near, hamiltonian[:, 1:], preferred_element_...  14.1 us
    ppermute x3, starting transfers between devices, with_halo(): lax.ppermute(lax.slice_in_dim(block, block.shape[dim] - width, None, axis...  8.79 us
  transfers between devices with their start and end apart: 9, of which 9 were waited for; matrix products, arithmetic and copies ran while one was open for 0% of the time, Pallas kernels for 0%

commit v1 on v0

v1 whole, which is shorter than its diff:
```python
import functools

import jax
import jax.numpy as jnp
from jax import lax
from jax.experimental import pallas as pl
from jax.experimental.pallas import tpu as pltpu
from jax.sharding import PartitionSpec as P

MESH = pl.DeviceIdType.MESH
CENTRE = 0.25
RADIUS = 0.75
F32, BF16 = jnp.float32, jnp.bfloat16
NT = (((1,), (1,)), ((), ()))
DMA = pltpu.SemaphoreType.DMA


def remote(src, dst, send, recv, **where):
    return pltpu.make_async_remote_copy(
        src_ref=src, dst_ref=dst, send_sem=send, recv_sem=recv, device_id=where, device_id_type=MESH
    )


def loop(n, body):
    lax.fori_loop(0, n, lambda i, c: (body(i), c)[1], 0)


def filter_kernel(
    ham_hbm, orb_ref, adj_ref, gram_out, filt_out, low_out,
    ham, lev0, lev1, lev2, lo0, hi0, lo1, hi1, lo2, hi2, part, low, filt, slab, zbuf, ybuf, gram,
    ham_sem, halo_send, halo_recv, ag_send, ag_recv, gg_send, gg_recv,
    red_send, red_recv, out_sem,
):
    level, halo = (lev0, lev1, lev2), ((lo0, hi0), (lo1, hi1), (lo2, hi2))
    space, orb = lax.axis_index("space"), lax.axis_index("orb")
    y, z = space // 8, space % 8
    chip, core = orb // 2, orb % 2
    after, before = (space + 1) % 64, (space + 63) % 64
    partner = chip * 2 + 1 - core
    right = ((chip + 1) % 4) * 2 + core
    left = ((chip + 3) % 4) * 2 + core
    cross = ((chip + 2) % 4) * 2 + core

    def load_ham(e):
        return pltpu.make_async_copy(ham_hbm.at[e], ham.at[e], ham_sem.at[e])

    loop(8, lambda e: load_ham(e).start())

    bar = pltpu.get_barrier_semaphore()
    for where in ({"space": after}, {"space": before}, {"orb": partner}, {"orb": right}, {"orb": left}):
        pl.semaphore_signal(bar, inc=1, device_id=where, device_id_type=MESH)
    for d in range(1, 8):
        pl.semaphore_signal(bar, inc=1, device_id={"space": y * 8 + (z + d) % 8}, device_id_type=MESH)
        pl.semaphore_signal(bar, inc=1, device_id={"space": ((y + d) % 8) * 8 + z}, device_id_type=MESH)
    pl.semaphore_wait(bar, 19)

    def halo_copy(n, side, e):
        src = orb_ref.at[:, pl.ds(pl.multiple_of(e * 256, 256), 256)] if n == 0 else level[n].at[e]
        return remote(src, halo[n][side].at[e], halo_send.at[n, side, e], halo_recv.at[n, side, e],
                      space=after if side == 0 else before)

    def start0(e):
        halo_copy(0, 0, e).start()
        halo_copy(0, 1, e).start()

    loop(8, start0)
    for e in range(8):
        level[0][e] = orb_ref[:, e * 256:(e + 1) * 256]

    def ag_copy(buf, n, send, recv, kind, t):
        if kind == 6:
            raise ValueError
        who = (orb, orb, orb, left, right, cross)[kind]
        dst = (partner, right, left, partner, partner, partner)[kind]
        slot = (0, 1, 2, 4, 5, 6)[kind]
        return remote(buf.at[t, who], buf.at[t, who], send.at[kind, t], recv.at[slot, t], orb=dst)

    def forward(buf, send, recv, t, to_right):
        who = left if to_right else right
        return remote(buf.at[t, who], buf.at[t, who], send.at[6, t], recv.at[3, t],
                      orb=right if to_right else left)

    def arrived(buf, send, recv, slot, t):
        who = (partner, left, right, cross, 0, 0, 0)[slot]
        remote(buf.at[t, who], buf.at[t, who], send.at[0, t], recv.at[slot, t], orb=partner).wait_recv()

    def ag_start(buf, n, send, recv, t):
        for kind in (1, 2, 0):
            ag_copy(buf, n, send, recv, kind, t).start()

    def ag_relay(buf, n, send, recv):
        def near(t, to_right):
            arrived(buf, send, recv, 1, t)
            if to_right:
                forward(buf, send, recv, t, True).start()
            ag_copy(buf, n, send, recv, 3, t).start()
            arrived(buf, send, recv, 2, t)
            if not to_right:
                forward(buf, send, recv, t, False).start()
            ag_copy(buf, n, send, recv, 4, t).start()

        def far(t):
            arrived(buf, send, recv, 3, t)
            ag_copy(buf, n, send, recv, 5, t).start()

        h = n // 2
        loop(h, lambda t: near(t, True))
        loop(n - h, lambda t: near(t + h, False))
        loop(n, far)

    def ag_rest(buf, send, recv, t):
        for slot in (0, 4, 5, 6):
            arrived(buf, send, recv, slot, t)

    def ag_drain(buf, n, send, recv):
        def body(t):
            for kind in range(6):
                ag_copy(buf, n, send, recv, kind, t).wait_send()
            forward(buf, send, recv, t, True).wait_send()
        loop(n, body)

    def dot(v, h):
        return lax.dot_general(v, h, NT, preferred_element_type=F32)

    for n in range(3):
        def inner(e, n=n):
            if n == 0:
                load_ham(e).wait()
            total = dot(level[n][e], ham[e, 0])
            for f in range(2, 6):
                total = total + dot(level[n][adj_ref[e, f] & 7], ham[e, f + 1])
            part[e] = total

        loop(8, inner)

        def landed(e, n=n):
            halo_copy(n, 0, e).wait_recv()
            halo_copy(n, 1, e).wait_recv()

        loop(8, landed)

        def outer(e, n=n):
            total = part[e] + dot(halo[n][0][adj_ref[e, 0] & 7], ham[e, 1])
            total = total + dot(halo[n][1][adj_ref[e, 1] & 7], ham[e, 2])
            total = (total - CENTRE * level[n][e].astype(F32)) * (1.0 / RADIUS)
            if n > 0:
                total = 2.0 * total - level[n - 1][e].astype(F32)
            if n < 2:
                level[n + 1][e] = total.astype(BF16)
                halo_copy(n + 1, 0, e).start()
                halo_copy(n + 1, 1, e).start()
            else:
                high = total.astype(BF16)
                filt[e, orb] = high
                low[e] = (total - high.astype(F32)).astype(BF16)
                ag_start(filt, 8, ag_send, ag_recv, e)

        loop(8, outer)

    ag_relay(filt, 8, ag_send, ag_recv)
    slab[...] = jnp.zeros_like(slab)

    def product(e):
        ag_rest(filt, ag_send, ag_recv, e)
        slab[...] += dot(filt[e, orb], filt[e].reshape(256, 256))

    loop(8, product)
    out_f = pltpu.make_async_copy(filt, filt_out, out_sem.at[0])
    out_f.start()
    out_l = pltpu.make_async_copy(low, low_out, out_sem.at[1])
    out_l.start()

    def red(stage, half, d):
        buf = zbuf if stage == half else ybuf
        mine = z if stage == half else y
        where = y * 8 + (z + d) % 8 if stage == half else ((y + d) % 8) * 8 + z
        return remote(buf.at[half, mine], buf.at[half, mine],
                      red_send.at[stage, half, d], red_recv.at[stage, half, d], space=where)

    order = (4, 3, 5, 2, 6, 1, 7)
    for stage in range(2):
        for half in range(2):
            buf = zbuf if stage == half else ybuf
            mine = z if stage == half else y
            if stage == 0:
                buf[half, mine] = slab[16 * half:16 * half + 16]
            else:
                prev = ybuf if stage == half else zbuf
                for d in order:
                    red(0, half, d).wait_recv()
                total = prev[half, 0]
                for i in range(1, 8):
                    total = total + prev[half, i]
                buf[half, mine] = total
            for d in order:
                red(stage, half, d).start()
    for half in range(2):
        prev = ybuf if half == 0 else zbuf
        for d in order:
            red(1, half, d).wait_recv()
        total = prev[half, 0]
        for i in range(1, 8):
            total = total + prev[half, i]
        gram[half, orb] = total
        ag_start(gram, 2, gg_send, gg_recv, half)
    ag_relay(gram, 2, gg_send, gg_recv)
    loop(2, lambda t: ag_rest(gram, gg_send, gg_recv, t))
    out_g = pltpu.make_async_copy(gram, gram_out, out_sem.at[2])
    out_g.start()

    for n in range(3):
        def sent(e, n=n):
            halo_copy(n, 0, e).wait_send()
            halo_copy(n, 1, e).wait_send()
        loop(8, sent)
    ag_drain(filt, 8, ag_send, ag_recv)
    for stage in range(2):
        for half in range(2):
            for d in order:
                red(stage, half, d).wait_send()
    ag_drain(gram, 2, gg_send, gg_recv)
    out_f.wait()
    out_l.wait()
    out_g.wait()


def filter_call(hamiltonian, orbitals, adjacency):
    anywhere = pl.BlockSpec(memory_space=pl.ANY)
    return pl.pallas_call(
        filter_kernel,
        out_shape=(
            jax.ShapeDtypeStruct((2, 8, 16, 256), F32),
            jax.ShapeDtypeStruct((8, 8, 32, 256), BF16),
            jax.ShapeDtypeStruct((8, 32, 256), BF16),
        ),
        in_specs=[anywhere, pl.BlockSpec(memory_space=pltpu.VMEM), pl.BlockSpec(memory_space=pltpu.SMEM)],
        out_specs=(anywhere, anywhere, anywhere),
        scratch_shapes=[
            pltpu.VMEM((8, 7, 256, 256), BF16),
            *[pltpu.VMEM((8, 32, 256), BF16)] * 9,
            pltpu.VMEM((8, 32, 256), F32),
            pltpu.VMEM((8, 32, 256), BF16),
            pltpu.VMEM((8, 8, 32, 256), BF16),
            pltpu.VMEM((32, 256), F32),
            pltpu.VMEM((2, 8, 16, 256), F32),
            pltpu.VMEM((2, 8, 16, 256), F32),
            pltpu.VMEM((2, 8, 16, 256), F32),
            DMA((8,)),
            DMA((3, 2, 8)), DMA((3, 2, 8)),
            DMA((7, 8)), DMA((7, 8)),
            DMA((7, 2)), DMA((7, 2)),
            DMA((2, 2, 8)), DMA((2, 2, 8)),
            DMA((3,)),
        ],
        compiler_params=pltpu.CompilerParams(
            collective_id=0, has_side_effects=True, vmem_limit_bytes=40 * 2**20
        ),
        name="filter",
    )(hamiltonian, orbitals, adjacency)


def shards(hamiltonian, orbitals, adjacency):
    gram, filt, low = filter_call(hamiltonian, orbitals, adjacency)
    gram = gram.transpose(1, 0, 2, 3).reshape(256, 256)
    lower = jnp.linalg.cholesky(gram)
    inverse = lax.linalg.triangular_solve(lower, jnp.eye(256, dtype=F32), left_side=True, lower=True)
    orb = lax.axis_index("orb")
    rows = lax.dynamic_slice_in_dim(inverse, orb * 32, 32, 0)
    mine = lax.dynamic_slice_in_dim(rows, orb * 32, 32, 1)
    whole = filt.astype(F32).reshape(8, 256, 256)
    basis = jnp.einsum("ro,eoc->rec", rows, whole, precision=lax.Precision.HIGHEST)
    basis = basis + jnp.einsum("ro,eoc->rec", mine, low.astype(F32), precision=lax.Precision.HIGHEST)
    return basis.reshape(32, 2048), lower.T


def solution(mesh):
    in_specs = (P("space", None, None, None), P("orb", "space"), P("space", None))
    out_specs = (P("orb", "space"), P())
    return jax.shard_map(shards, mesh=mesh, in_specs=in_specs, out_specs=out_specs, check_vma=False)
```

time: 436 us -> 134 us (0.31)
  waiting for transfers between devices: 284 us -> 0 us
  Pallas kernels: 0 us -> 64.9 us
  starting transfers between devices: 46.6 us -> 0 us
  matrix products: 21.5 us -> 2.24 us
  between operations: 15.5 us -> 2.09 us
    psum x1 -> x0, waiting for transfers between devices: 266 us -> none  [shards(): gram = lax.psum(partial_gram, ('space', 'orb'))]
    pallas_call x0 -> x1, Pallas kernels: none -> 64.9 us  [filter_call(): pl.pallas_call(filter_kernel, out_shape=(jax.ShapeDtypeStruct((2, 8, 16,...]
    ppermute x6 -> x0, starting transfers between devices: 34.7 us -> none  [the longest x3 25.9 us: with_halo(): lax.ppermute(lax.slice_in_dim(block, 0, width, axis=dim), axis, backward)]
    dot_general x7 -> x2, matrix products: 20.2 us -> 0.94 us  [the longest x1 0.61 us: shards(): jnp.einsum('ro,eoc->rec', rows, whole, precision=lax.Precision.HIGHEST)]
    all_to_all x2 -> x0, waiting for transfers between devices: 12.1 us -> none  [the longest x1 6.46 us: shards(): lax.all_to_all(filtered, 'orb', split_axis=1, concat_axis=0, tiled=True)]
    all_to_all x2 -> x0, starting transfers between devices: 11.9 us -> none  [the longest x1 7.82 us: shards(): lax.all_to_all(filtered, 'orb', split_axis=1, concat_axis=0, tiled=True)]
    ppermute x6 -> x0, waiting for transfers between devices: 5.51 us -> none  [the longest x3 4.03 us: with_halo(): lax.ppermute(lax.slice_in_dim(block, 0, width, axis=dim), axis, backward)]
    unnamed x3 -> x7, local copies, waits for them, and re-layouts: 0.84 us -> 5.5 us
  transfers between devices with their start and end apart: 9 -> 0, of which waited for: 9 -> 0; matrix products, arithmetic and copies ran while one was open for 0% -> 0% of each run, Pallas kernels for 0% -> 0%
where the time goes in v1:
time: 134 us
  Pallas kernels  64.9 us (48%)
  other arithmetic  53.9 us (40%)
  local copies, waits for them, and re-layouts  10.5 us (8%)
  matrix products  2.24 us (2%)
  between operations  2.09 us (2%)
    pallas_call x1, Pallas kernels, filter_call(): pl.pallas_call(filter_kernel, out_shape=(jax.ShapeDtypeStruct((2, 8, 16,...  64.9 us
    another operation x6, other arithmetic, shards(): lower = jnp.linalg.cholesky(gram)  34 us
    another operation x2, other arithmetic, shards(): lax.linalg.triangular_solve(lower, jnp.eye(256, dtype=F32), left_side=Tru...  19.9 us
    unnamed x7, local copies, waits for them, and re-layouts  5.5 us
    another operation x6, local copies, waits for them, and re-layouts  4.06 us

profile of v1, /device:TPU:1, one launch (start us, length us, event | category | flops | bytes accessed | tf_op | source)
XLA Modules:
  0.0 133.8 jit_solution(13743064154764421524)
XLA Ops:
  0.6 0.0 copy-start
  0.6 3.1 %copy-done = bf16[8,7,256,256]{3,2,1,0:T(8,128)(2,1)S(1)} copy-done((bf16[8,7,256,256]{3,2,1,0:T(8,128)(2,1)S(1)}, bf16[8,7,256,256]{3,2,1,0:T(8,128)(2,1)}, u32[]{:S(2)}) %copy-start) | copy-done | bytes 7340056
  3.7 0.0 copy-start.1
  3.7 0.9 copy-done.1
  4.6 0.0 copy-start.2
  4.6 0.7 copy-done.2
  5.3 64.9 %filter.1 = (f32[2,8,16,256]{3,2,1,0:T(8,128)S(1)}, bf16[8,8,32,256]{3,2,1,0:T(8,128)(2,1)S(1)}, bf16[8,32,256]{2,1,0:T(8,128)(2,1)S(1)}) custom-call(bf16[8,7,256,256]{3,2,1,0:T(8,128)(2,1)S(1)} %copy-done, bf16[32,2048]{1,0:T(8,128)(2,1)S(1)} %copy-done.1, s32[8,6]{1,0:T(8,128)S(1)} %copy-done.2), custom_call_target="tpu_custom_call" | custom-call | tf_op jit(solution)/shard_map/filter/pallas_call | solution.py:229
  70.3 0.1 copy.9
  70.5 11.7 %cholesky.50 = f32[128,128]{1,0:T(8,128)S(1)} custom-call(f32[128,128]{1,0:T(8,128)S(1)} %cholesky.118), custom_call_target="Cholesky" | custom-call | tf_op jit(solution)/shard_map/jit(cholesky)/cholesky | solution.py:265
  82.2 9.8 %custom-call.14 = f32[1,128,128]{1,2,0:T(8,128)S(1)} custom-call(f32[1,128,128]{2,1,0:T(8,128)S(1)} %get-tuple-element.35), custom_call_target="InvertDiagBlocksLowerTriangular" | custom-call | tf_op jit(solution)/shard_map/jit(cholesky)/cholesky | solution.py:265
  92.1 0.2 constant_dynamic-update-slice_fusion
  92.3 0.3 convolution_subtract_fusion.1
  92.6 11.7 %cholesky.105 = f32[128,128]{1,0:T(8,128)S(1)} custom-call(f32[128,128]{1,0:T(8,128)S(1)} %convolution_subtract_fusion.1), custom_call_target="Cholesky" | custom-call | tf_op jit(solution)/shard_map/jit(cholesky)/cholesky | solution.py:265
  104.3 0.6 compare_reduce_fusion
  106.3 0.1 triangular_solve.63
  106.4 4.1 %while.1 = (s32[]{:T(128)}, f32[256,256]{1,0:T(8,128)S(1)}, s32[2,2]{1,0:T(2,128)S(1)}, f32[2,128,128]{2,1,0:T(8,128)S(1)}, s32[]{:T(128)}) while((s32[]{:T(128)}, f32[256,256]{1,0:T(8,128)S(1)}, s32[2,2]{1,0:T(2,128)S(1)}, f32[2,128,128]{2,1,0:T(8,128)S(1)}, s32[]{:T(128)}) %tuple.30), condition=%wide.while_cond, body=%wide.while_body.sunk | while | flops 2 | bytes 131181 | solution.py:266
  106.4 0.6 fusion.29
  107.0 1.4 %bitcast_dynamic-update-slice_fusion.2 = f32[2,128,128]{2,1,0:T(8,128)S(1)} fusion(f32[2,128,128]{2,1,0:T(8,128)S(1)} %get-tuple-element.77, s32[]{:T(128)} %get-tuple-element.74, f32[256,256]{1,0:T(8,128)S(1)} %get-tuple-element.80, s32[]{:T(128)} %bitcast.46, s32[]{:T(128)} %bitcast.47), kind=kLoop, calls=%fused_computation.clone.1 | loop fusion | bytes 131084 | tf_op jit(solution)/shard_map/triangular_solve
  108.5 0.6 fusion.29
  109.0 1.4 %bitcast_dynamic-update-slice_fusion.2 = f32[2,128,128]{2,1,0:T(8,128)S(1)} fusion(f32[2,128,128]{2,1,0:T(8,128)S(1)} %get-tuple-element.77, s32[]{:T(128)} %get-tuple-element.74, f32[256,256]{1,0:T(8,128)S(1)} %get-tuple-element.80, s32[]{:T(128)} %bitcast.46, s32[]{:T(128)} %bitcast.47), kind=kLoop, calls=%fused_computation.clone.1 | loop fusion | bytes 131084 | tf_op jit(solution)/shard_map/triangular_solve
  110.5 19.9 %custom-call.15 = f32[2,128,128]{1,2,0:T(8,128)S(1)} custom-call(f32[2,128,128]{2,1,0:T(8,128)S(1)} %get-tuple-element.15), custom_call_target="InvertDiagBlocksLowerTriangular" | custom-call | tf_op jit(solution)/shard_map/triangular_solve | solution.py:266
  130.4 0.3 fusion.4
  130.7 0.3 convolution_subtract_fusion
  130.9 0.3 fusion.7
  131.2 0.6 fusion.13
  131.9 0.3 fusion
  132.2 0.7 copy.12
  132.9 0.8 copy.11
  (12 shorter events, 0.2 us)
Async XLA Ops:
  0.6 3.1 %copy-start = (bf16[8,7,256,256]{3,2,1,0:T(8,128)(2,1)S(1)}, bf16[8,7,256,256]{3,2,1,0:T(8,128)(2,1)}, u32[]{:S(2)}) copy-start(bf16[8,7,256,256]{3,2,1,0:T(8,128)(2,1)} %ham_hbm.1) | copy-start | bytes 22020100
  3.7 0.9 copy-start.1
  4.6 0.7 copy-start.2

commit v2 on v1

v2 whole, which is shorter than its diff:
```python
import functools

import jax
import jax.numpy as jnp
from jax import lax
from jax.experimental import pallas as pl
from jax.experimental.pallas import tpu as pltpu
from jax.sharding import PartitionSpec as P

MESH = pl.DeviceIdType.MESH
CENTRE = 0.25
RADIUS = 0.75
F32, BF16 = jnp.float32, jnp.bfloat16
NT = (((1,), (1,)), ((), ()))
DMA = pltpu.SemaphoreType.DMA


def remote(src, dst, send, recv, **where):
    return pltpu.make_async_remote_copy(
        src_ref=src, dst_ref=dst, send_sem=send, recv_sem=recv, device_id=where, device_id_type=MESH
    )


def loop(n, body):
    lax.fori_loop(0, n, lambda i, c: (body(i), c)[1], 0)


def filter_kernel(
    ham_hbm, orb_hbm, adj_hbm, gram_a_out, gram_b_out, filt_out, low_out,
    ham, adj, lev0, lev1, lev2, lo0, hi0, lo1, hi1, lo2, hi2, part, low, filt, near_sum, far_sum,
    za, ya, yb, zb, gram_a, gram_b,
    ham_sem, in_sem, token, halo_send, halo_recv, ag_send, ag_recv, gg_send, gg_recv,
    red_send, red_recv, out_sem,
):
    level, halo = (lev0, lev1, lev2), ((lo0, hi0), (lo1, hi1), (lo2, hi2))
    space, orb = lax.axis_index("space"), lax.axis_index("orb")
    y, z = space // 8, space % 8
    chip, core = orb // 2, orb % 2
    after, before = (space + 1) % 64, (space + 63) % 64
    chip_r, chip_l, chip_x = (chip + 1) % 4, (chip + 3) % 4, (chip + 2) % 4
    partner = chip * 2 + 1 - core
    right, left = chip_r * 2 + core, chip_l * 2 + core
    left_to = chip_l * 2 + (core + chip_l // 2) % 2
    from_l = left
    from_r = chip_r * 2 + (core + chip // 2) % 2
    from_x = chip_x * 2 + core
    from_y = chip_x * 2 + (core + chip_r // 2) % 2
    pair = chip * 2 + (core + 1 + chip // 2) % 2

    def load_ham(e):
        return pltpu.make_async_copy(ham_hbm.at[e], ham.at[e], ham_sem.at[e])

    def load_level(e):
        src = orb_hbm.at[:, pl.ds(pl.multiple_of(e * 256, 256), 256)]
        return pltpu.make_async_copy(src, lev0.at[e], in_sem.at[e])

    load_adj = pltpu.make_async_copy(adj_hbm, adj, in_sem.at[8])

    close = (
        {"space": after}, {"space": before},
        {"space": y * 8 + (z + 1) % 8}, {"space": y * 8 + (z + 7) % 8},
        {"space": (y + 1) % 8 * 8 + z}, {"space": (y + 7) % 8 * 8 + z},
        {"orb": partner}, {"orb": chip_r * 2}, {"orb": chip_r * 2 + 1}, {"orb": chip_l * 2}, {"orb": chip_l * 2 + 1},
    )
    bar = pltpu.get_barrier_semaphore()
    for where in close:
        pl.semaphore_signal(bar, inc=1, device_id=where, device_id_type=MESH)
    load_adj.start()
    loop(8, lambda e: load_level(e).start())
    loop(8, lambda e: load_ham(e).start())
    pl.semaphore_wait(bar, len(close))

    def halo_copy(n, side, e):
        src = orb_hbm.at[:, pl.ds(pl.multiple_of(e * 256, 256), 256)] if n == 0 else level[n].at[e]
        return remote(src, halo[n][side].at[e], halo_send.at[n, side, e], halo_recv.at[n, side, e],
                      space=after if side == 0 else before)

    def start0(e):
        halo_copy(0, 0, e).start()
        halo_copy(0, 1, e).start()

    loop(8, start0)

    def pass_token(n):
        for where in close:
            pl.semaphore_signal(token.at[n], inc=1, device_id=where, device_id_type=MESH)

    def take_token(n):
        pl.semaphore_wait(token.at[n], len(close))

    pass_token(0)

    def gather(kind, t):
        who = (orb, orb, orb, from_l, from_r, from_x, from_l, from_r, from_y)[kind]
        dst = (right, left_to, partner, partner, partner, partner, right, left, partner)[kind]
        send = (0, 1, 2, 3, 4, 5, 6, 6, 5)[kind]
        slot = (0, 1, 2, 3, 4, 5, 6, 6, 5)[kind]
        return remote(filt.at[t, who], filt.at[t, who], ag_send.at[send, t], ag_recv.at[slot, t], orb=dst)

    def arrived(slot, t):
        remote(filt.at[t, orb], filt.at[t, orb], ag_send.at[0, t], ag_recv.at[slot, t], orb=partner).wait_recv()

    def dot(v, h):
        return lax.dot_general(v, h, NT, preferred_element_type=F32)

    load_adj.wait()
    loop(8, lambda e: load_level(e).wait())
    for n in range(3):
        def inner(e, n=n):
            if n == 0:
                load_ham(e).wait()
            total = dot(level[n][e], ham[e, 0])
            for f in range(2, 6):
                total = total + dot(level[n][adj[e, f] & 7], ham[e, f + 1])
            part[e] = total

        loop(8, inner)
        take_token(n)
        if n < 2:
            pass_token(n + 1)

        def landed(e, n=n):
            halo_copy(n, 0, e).wait_recv()
            halo_copy(n, 1, e).wait_recv()

        loop(8, landed)

        def outer(e, n=n):
            total = part[e] + dot(halo[n][0][adj[e, 0] & 7], ham[e, 1])
            total = total + dot(halo[n][1][adj[e, 1] & 7], ham[e, 2])
            total = (total - CENTRE * level[n][e].astype(F32)) * (1.0 / RADIUS)
            if n > 0:
                total = 2.0 * total - level[n - 1][e].astype(F32)
            if n < 2:
                level[n + 1][e] = total.astype(BF16)
                halo_copy(n + 1, 0, e).start()
                halo_copy(n + 1, 1, e).start()
            else:
                high = total.astype(BF16)
                filt[e, orb] = high
                low[e] = (total - high.astype(F32)).astype(BF16)
                for kind in range(3):
                    gather(kind, e).start()

        loop(8, outer)

    near_sum[...] = jnp.zeros_like(near_sum)
    far_sum[...] = jnp.zeros_like(far_sum)

    def product(t, first):
        arrived(0, t)
        if first:
            gather(6, t).start()
        gather(3, t).start()
        arrived(1, t)
        if not first:
            gather(7, t).start()
        gather(4, t).start()
        arrived(2, t)
        mine, west = filt[t, orb], filt[t, from_l]
        near_sum[...] += dot(mine, jnp.concatenate([mine, filt[t, partner], west, mine], axis=0))
        far_sum[...] += dot(filt[t, from_r], jnp.concatenate([west, west, west, filt[t, pair]], axis=0))

    loop(4, lambda t: product(t, True))
    loop(4, lambda t: product(t + 4, False))

    order = (4, 3, 5, 2, 6, 1, 7)
    bufs = ((za, ya), (yb, zb))

    def red(stage, half, d):
        along_z = stage == half
        buf = bufs[half][stage]
        mine = z if along_z else y
        where = y * 8 + (z + d) % 8 if along_z else ((y + d) % 8) * 8 + z
        return remote(buf.at[mine], buf.at[mine],
                      red_send.at[stage, half, d], red_recv.at[stage, half, d], space=where)

    def summed(stage, half):
        buf = bufs[half][stage]
        for d in order:
            red(stage, half, d).wait_recv()
        total = buf[0]
        for i in range(1, 8):
            total = total + buf[i]
        return total

    lane = lax.broadcasted_iota(jnp.int32, (32, 128), 1)
    main = jnp.where(lane < 96, near_sum[...], far_sum[...])
    lane8 = lax.broadcasted_iota(jnp.int32, (8, 128), 1)
    fold = far_sum[0:8]
    fold = jnp.where(lane8 < 32, fold, far_sum[8:16])
    fold = jnp.where(lane8 < 64, fold, far_sum[16:24])
    rest = jnp.where(lane8 < 96, fold, pltpu.roll(far_sum[24:32], 96, 1))
    za[z] = main[:24]
    yb[y, 0:8] = main[24:]
    yb[y, 8:16] = rest
    for half in range(2):
        for d in order:
            red(0, half, d).start()
    for half in range(2):
        total = summed(0, half)
        if half == 0:
            ya[y] = total
        else:
            zb[z] = total
        for d in order:
            red(1, half, d).start()

    def across_first(t):
        arrived(6, t)
        gather(5, t).start()

    def across_second(t):
        arrived(6, t + 4)
        gather(8, t + 4).start()

    loop(4, across_first)
    loop(4, across_second)

    def share(half, d):
        buf = gram_b if half else gram_a
        return remote(buf.at[orb], buf.at[orb], gg_send.at[half, d], gg_recv.at[half, d], orb=(orb + d) % 8)

    for half in range(2):
        total = summed(1, half)
        (gram_b if half else gram_a)[orb] = total
        for d in order:
            share(half, d).start()

    def rest_landed(t):
        for slot in (3, 4, 5):
            arrived(slot, t)

    loop(8, rest_landed)
    out_f = pltpu.make_async_copy(filt, filt_out, out_sem.at[0])
    out_f.start()
    out_l = pltpu.make_async_copy(low, low_out, out_sem.at[1])
    out_l.start()
    for n in range(3):
        def sent(e, n=n):
            halo_copy(n, 0, e).wait_send()
            halo_copy(n, 1, e).wait_send()
        loop(8, sent)

    def gathered(t):
        for kind in range(7):
            gather(kind, t).wait_send()

    loop(8, gathered)
    for stage in range(2):
        for half in range(2):
            for d in order:
                red(stage, half, d).wait_send()
    for half in range(2):
        for d in order:
            share(half, d).wait_recv()
    out_a = pltpu.make_async_copy(gram_a, gram_a_out, out_sem.at[2])
    out_a.start()
    out_b = pltpu.make_async_copy(gram_b, gram_b_out, out_sem.at[3])
    out_b.start()
    for half in range(2):
        for d in order:
            share(half, d).wait_send()
    for out in (out_f, out_l, out_a, out_b):
        out.wait()


def filter_call(hamiltonian, orbitals, adjacency):
    anywhere = pl.BlockSpec(memory_space=pl.ANY)
    outside = pl.BlockSpec(memory_space=pltpu.HBM)
    return pl.pallas_call(
        filter_kernel,
        out_shape=(
            jax.ShapeDtypeStruct((8, 24, 128), F32),
            jax.ShapeDtypeStruct((8, 16, 128), F32),
            jax.ShapeDtypeStruct((8, 8, 32, 256), BF16),
            jax.ShapeDtypeStruct((8, 32, 256), BF16),
        ),
        in_specs=[outside, outside, outside],
        out_specs=(anywhere,) * 4,
        scratch_shapes=[
            pltpu.VMEM((8, 7, 256, 256), BF16),
            pltpu.SMEM((8, 6), jnp.int32),
            *[pltpu.VMEM((8, 32, 256), BF16)] * 9,
            pltpu.VMEM((8, 32, 256), F32),
            pltpu.VMEM((8, 32, 256), BF16),
            pltpu.VMEM((8, 8, 32, 256), BF16),
            pltpu.VMEM((32, 128), F32), pltpu.VMEM((32, 128), F32),
            *[pltpu.VMEM((8, 24, 128), F32)] * 2,
            *[pltpu.VMEM((8, 16, 128), F32)] * 2,
            pltpu.VMEM((8, 24, 128), F32), pltpu.VMEM((8, 16, 128), F32),
            DMA((8,)), DMA((9,)), pltpu.SemaphoreType.REGULAR((3,)),
            DMA((3, 2, 8)), DMA((3, 2, 8)),
            DMA((7, 8)), DMA((7, 8)),
            DMA((2, 8)), DMA((2, 8)),
            DMA((2, 2, 8)), DMA((2, 2, 8)),
            DMA((4,)),
        ],
        compiler_params=pltpu.CompilerParams(
            collective_id=0, has_side_effects=True, vmem_limit_bytes=40 * 2**20
        ),
        name="filter",
    )(hamiltonian, orbitals, adjacency)


TN = (((0,), (0,)), ((), ()))
NN = (((1,), (0,)), ((), ()))


def exact_dot(a, b, dims):
    return lax.dot_general(a, b, dims, precision=lax.Precision.HIGHEST, preferred_element_type=F32)


def spread(x, i, j):
    return jnp.broadcast_to(x[i:i + 1, j:j + 1], (8, 128))


def factor_block(tiles):
    sub = lax.broadcasted_iota(jnp.int32, (8, 128), 0)
    tiles = list(tiles)
    done = []
    for s in range(8):
        tile = tiles[s]
        at = [[spread(tile, i, 8 * s + j) if j >= i else None for j in range(8)] for i in range(8)]
        rows = [jnp.broadcast_to(tile[k:k + 1, :], (8, 128)) for k in range(8)]
        cols = {g: [jnp.broadcast_to(tiles[g][:, 8 * s + k:8 * s + k + 1], (8, 128)) for k in range(8)]
                for g in range(s + 1, 8)}
        for k in range(8):
            r = lax.rsqrt(at[k][k])
            r = r * (1.5 - 0.5 * at[k][k] * r * r)
            rows[k] = rows[k] * r
            for j in range(k + 1, 8):
                at[k][j] = at[k][j] * r
            for g in cols:
                cols[g][k] = cols[g][k] * r
            for i in range(k + 1, 8):
                for j in range(i, 8):
                    at[i][j] = at[i][j] - at[k][i] * at[k][j]
                rows[i] = rows[i] - at[k][i] * rows[k]
                for g in cols:
                    cols[g][i] = cols[g][i] - at[k][i] * cols[g][k]
        for g in cols:
            t = tiles[g]
            for k in range(8):
                t = t - cols[g][k] * rows[k]
            tiles[g] = t
        out = rows[0]
        for k in range(1, 8):
            out = jnp.where(sub == k, rows[k], out)
        done.append(out)
    return jnp.concatenate(done, axis=0)


def finish_kernel(gram_a_ref, gram_b_ref, filt_hbm, low_hbm, basis_ref, factor_ref, work, rest, inv, filt, low, sem):
    load_f = pltpu.make_async_copy(filt_hbm, filt, sem.at[0])
    load_f.start()
    load_l = pltpu.make_async_copy(low_hbm, low, sem.at[1])
    load_l.start()
    def place(i, j, block):
        if i // 2 > j // 2:
            i, j, block = j, i, block.T
        work[32 * i:32 * i + 32, 32 * j:32 * j + 32] = block

    for o in range(8):
        chip, core = o // 2, o % 2
        left = (chip + 3) % 4 * 2 + core
        right = (chip + 1) % 4 * 2 + (core + chip // 2) % 2
        pair = chip * 2 + (core + 1 + chip // 2) % 2
        top = jnp.concatenate([gram_a_ref[o], gram_b_ref[o, 0:8]], axis=0)
        fold = gram_b_ref[o, 8:16]
        place(o, o, top[:, :32])
        place(o, o ^ 1, top[:, 32:64])
        place(o, left, top[:, 64:96])
        place(right, pair, top[:, 96:])
        place(right, left, jnp.concatenate([fold[:, 32 * q:32 * q + 32] for q in range(4)], axis=0))
    eye = (lax.broadcasted_iota(jnp.int32, (64, 64), 0) == lax.broadcasted_iota(jnp.int32, (64, 64), 1)).astype(F32)
    upper = lax.broadcasted_iota(jnp.int32, (64, 64), 0) <= lax.broadcasted_iota(jnp.int32, (64, 64), 1)
    lower = lax.broadcasted_iota(jnp.int32, (64, 64), 0) >= lax.broadcasted_iota(jnp.int32, (64, 64), 1)
    rest[...] = jnp.zeros_like(rest)
    inv[...] = jnp.zeros_like(inv)
    factor_ref[...] = jnp.zeros_like(factor_ref)
    for p in range(4):
        a, b = 64 * p, 64 * p + 64
        block = jnp.concatenate([work[a:b, a:b], eye], axis=1)
        solved = factor_block([block[8 * s:8 * s + 8] for s in range(8)])
        factor_ref[a:b, a:b] = jnp.where(upper, solved[:, :64], 0.0)
        own = jnp.where(lower, solved[:, 64:], 0.0)
        inv[a:b, a:b] = own
        if p > 0:
            inv[a:b, :a] = exact_dot(own, rest[a:b, :a], NN)
        if p < 3:
            u = exact_dot(own, work[a:b, b:], NN)
            factor_ref[a:b, b:] = u
            work[b:, b:] = work[b:, b:] - exact_dot(u, u, TN)
            rest[b:, :b] = rest[b:, :b] - exact_dot(u, inv[a:b, :b], TN)
    orb = lax.axis_index("orb")
    mine = inv[pl.ds(pl.multiple_of(orb * 32, 32), 32), :]
    high = mine.astype(BF16)
    left = mine - high.astype(F32)
    mid = left.astype(BF16)
    tail = (left - mid.astype(F32)).astype(BF16)
    stack = jnp.concatenate([high, mid, tail], axis=0)
    here = pltpu.roll(mine, (256 - orb * 32) % 256, 1)[:, :32].astype(BF16)
    load_f.wait()
    load_l.wait()

    for e in range(8):
        d = lax.dot_general(stack, filt[e].reshape(256, 256), NN, preferred_element_type=F32)
        c = lax.dot_general(here, low[e], NN, preferred_element_type=F32)
        basis_ref[:, e * 256:(e + 1) * 256] = d[:32] + (d[32:64] + (d[64:] + c))


def finish_call(gram_a, gram_b, filt, low):
    anywhere = pl.BlockSpec(memory_space=pl.ANY)
    vmem = pl.BlockSpec(memory_space=pltpu.VMEM)
    return pl.pallas_call(
        finish_kernel,
        out_shape=(jax.ShapeDtypeStruct((32, 2048), F32), jax.ShapeDtypeStruct((256, 256), F32)),
        in_specs=[vmem, vmem, anywhere, anywhere],
        out_specs=(vmem, vmem),
        scratch_shapes=[
            pltpu.VMEM((256, 256), F32), pltpu.VMEM((256, 256), F32), pltpu.VMEM((256, 256), F32),
            pltpu.VMEM((8, 8, 32, 256), BF16), pltpu.VMEM((8, 32, 256), BF16), DMA((2,)),
        ],
        compiler_params=pltpu.CompilerParams(vmem_limit_bytes=40 * 2**20),
        name="finish",
    )(gram_a, gram_b, filt, low)


def shards(hamiltonian, orbitals, adjacency):
    return finish_call(*filter_call(hamiltonian, orbitals, adjacency))


def solution(mesh):
    in_specs = (P("space", None, None, None), P("orb", "space"), P("space", None))
    out_specs = (P("orb", "space"), P())
    return jax.shard_map(shards, mesh=mesh, in_specs=in_specs, out_specs=out_specs, check_vma=False)
```

time: 134 us -> 72 us (0.54)
  other arithmetic: 53.9 us -> 0 us
  local copies, waits for them, and re-layouts: 10.5 us -> 4.67 us
  matrix products: 2.24 us -> 0 us
  Pallas kernels: 64.9 us -> 66.5 us
  between operations: 2.09 us -> 0.65 us
    another operation x8 -> x0, other arithmetic: 53.8 us -> none  [the longest x6 34 us: shards(): lower = jnp.linalg.cholesky(gram)]
    another operation x9 -> x0, local copies, waits for them, and re-layouts: 4.16 us -> none
    pallas_call x1 -> x2, Pallas kernels: 64.9 us -> 66.5 us  [the longest x1 53.2 us: filter_call(): pl.pallas_call(filter_kernel, out_shape=(jax.ShapeDtypeStruct((8, 24, 128...]
    unnamed x7 -> x6, local copies, waits for them, and re-layouts: 5.5 us -> 4.67 us
where the time goes in v2:
time: 72 us; the launch traced here: 71.8 us
  Pallas kernels  66.5 us (92%)
  local copies, waits for them, and re-layouts  4.67 us (6%)
    pallas_call x1, Pallas kernels, filter_call(): pl.pallas_call(filter_kernel, out_shape=(jax.ShapeDtypeStruct((8, 24, 128...  53.2 us
    pallas_call x1, Pallas kernels, finish_call(): pl.pallas_call(finish_kernel, out_shape=(jax.ShapeDtypeStruct((32, 2048),...  13.3 us
    unnamed x6, local copies, waits for them, and re-layouts  4.67 us

profile of v2, /device:TPU:1, one launch (start us, length us, event | category | flops | bytes accessed | tf_op | source)
XLA Modules:
  0.0 71.8 jit_solution(15215040293718777131)
XLA Ops:
  0.6 0.0 copy-start
  0.6 3.1 %copy-done = bf16[8,7,256,256]{3,2,1,0:T(8,128)(2,1)S(1)} copy-done((bf16[8,7,256,256]{3,2,1,0:T(8,128)(2,1)S(1)}, bf16[8,7,256,256]{3,2,1,0:T(8,128)(2,1)}, u32[]{:S(2)}) %copy-start) | copy-done | bytes 7340056
  3.7 0.0 copy-start.1
  3.7 0.9 %copy-done.1 = bf16[32,2048]{1,0:T(8,128)(2,1)S(1)} copy-done((bf16[32,2048]{1,0:T(8,128)(2,1)S(1)}, bf16[32,2048]{1,0:T(8,128)(2,1)}, u32[]{:S(2)}) %copy-start.1) | copy-done | bytes 131096
  4.6 0.0 copy-start.2
  4.6 0.7 copy-done.2
  5.3 53.2 %filter.1 = (f32[8,24,128]{2,1,0:T(8,128)S(1)}, f32[8,16,128]{2,1,0:T(8,128)S(1)}, bf16[8,8,32,256]{3,2,1,0:T(8,128)(2,1)S(1)}, bf16[8,32,256]{2,1,0:T(8,128)(2,1)S(1)}) custom-call(bf16[8,7,256,256]{3,2,1,0:T(8,128)(2,1)S(1)} %copy-done, bf16[32,2048]{1,0:T(8,128)(2,1)S(1)} %copy-done.1, s32[8,6]{1,0:T(8,128)S(1)} %copy-done.2), custom_call_target="tpu_custom_call" | custom-call | tf_op jit(solution)/shard_map/filter/pallas_call | solution.py:271
  58.5 13.3 %finish.1 = (f32[32,2048]{1,0:T(8,128)}, f32[256,256]{1,0:T(8,128)}) custom-call(f32[8,24,128]{2,1,0:T(8,128)S(1)} %get-tuple-element.6.gram_a_ref, f32[8,16,128]{2,1,0:T(8,128)S(1)} %get-tuple-element.7.gram_b_ref, bf16[8,8,32,256]{3,2,1,0:T(8,128)(2,1)S(1)} %get-tuple-element.8.filt_hbm, bf16[8,32,256]{2,1,0:T(8,128)(2,1)S(1)} %get-tuple-element.9.low_hbm), custom_call_target="tpu_custom_call" | custom-call | tf_op jit(solution)/shard_map/finish/pallas_call | solution.py:416
Async XLA Ops:
  0.6 3.1 %copy-start = (bf16[8,7,256,256]{3,2,1,0:T(8,128)(2,1)S(1)}, bf16[8,7,256,256]{3,2,1,0:T(8,128)(2,1)}, u32[]{:S(2)}) copy-start(bf16[8,7,256,256]{3,2,1,0:T(8,128)(2,1)} %ham_hbm.1) | copy-start | bytes 22020100
  3.7 0.9 %copy-start.1 = (bf16[32,2048]{1,0:T(8,128)(2,1)S(1)}, bf16[32,2048]{1,0:T(8,128)(2,1)}, u32[]{:S(2)}) copy-start(bf16[32,2048]{1,0:T(8,128)(2,1)} %orb_hbm.1) | copy-start | bytes 393220
  4.6 0.7 copy-start.2

commit v3 on v2

--- a/solution.py
+++ b/solution.py
@@ -125,44 +125,51 @@
 
         loop(8, landed)
 
-        def outer(e, n=n):
-            total = part[e] + dot(halo[n][0][adj[e, 0] & 7], ham[e, 1])
-            total = total + dot(halo[n][1][adj[e, 1] & 7], ham[e, 2])
-            total = (total - CENTRE * level[n][e].astype(F32)) * (1.0 / RADIUS)
-            if n > 0:
-                total = 2.0 * total - level[n - 1][e].astype(F32)
-            if n < 2:
-                level[n + 1][e] = total.astype(BF16)
-                halo_copy(n + 1, 0, e).start()
-                halo_copy(n + 1, 1, e).start()
-            else:
-                high = total.astype(BF16)
-                filt[e, orb] = high
-                low[e] = (total - high.astype(F32)).astype(BF16)
-                for kind in range(3):
-                    gather(kind, e).start()
-
-        loop(8, outer)
+        def outer(group, n=n):
+            ids = [group * 4 + i for i in range(4)]
+            totals = []
+            for e in ids:
+                total = part[e] + dot(halo[n][0][adj[e, 0] & 7], ham[e, 1])
+                total = total + dot(halo[n][1][adj[e, 1] & 7], ham[e, 2])
+                total = (total - CENTRE * level[n][e].astype(F32)) * (1.0 / RADIUS)
+                if n > 0:
+                    total = 2.0 * total - level[n - 1][e].astype(F32)
+                totals.append(total)
+            for e, total in zip(ids, totals):
+                if n < 2:
+                    level[n + 1][e] = total.astype(BF16)
+                else:
+                    high = total.astype(BF16)
+                    filt[e, orb] = high
+                    low[e] = (total - high.astype(F32)).astype(BF16)
+            for e in ids:
+                if n < 2:
+                    halo_copy(n + 1, 0, e).start()
+                    halo_copy(n + 1, 1, e).start()
+                else:
+                    for kind in range(3):
+                        gather(kind, e).start()
+
+        loop(2, outer)
 
     near_sum[...] = jnp.zeros_like(near_sum)
     far_sum[...] = jnp.zeros_like(far_sum)
 
-    def product(t, first):
-        arrived(0, t)
-        if first:
-            gather(6, t).start()
-        gather(3, t).start()
-        arrived(1, t)
-        if not first:
-            gather(7, t).start()
-        gather(4, t).start()
-        arrived(2, t)
-        mine, west = filt[t, orb], filt[t, from_l]
-        near_sum[...] += dot(mine, jnp.concatenate([mine, filt[t, partner], west, mine], axis=0))
-        far_sum[...] += dot(filt[t, from_r], jnp.concatenate([west, west, west, filt[t, pair]], axis=0))
-
-    loop(4, lambda t: product(t, True))
-    loop(4, lambda t: product(t + 4, False))
+    def product(half):
+        mine, mate, west, east, twin = [], [], [], [], []
+        for t in [half * 2 + i for i in range(2)]:
+            for slot in range(3):
+                arrived(slot, t)
+            mine.append(filt[t, orb])
+            mate.append(filt[t, partner])
+            west.append(filt[t, from_l])
+            east.append(filt[t, from_r])
+            twin.append(filt[t, pair])
+        mine, mate, west, east, twin = (jnp.concatenate(x, axis=1) for x in (mine, mate, west, east, twin))
+        near_sum[...] += dot(mine, jnp.concatenate([mine, mate, west, mine], axis=0))
+        far_sum[...] += dot(east, jnp.concatenate([west, west, west, twin], axis=0))
+
+    loop(4, product)
 
     order = (4, 3, 5, 2, 6, 1, 7)
     bufs = ((za, ya), (yb, zb))
@@ -197,6 +204,17 @@
     for half in range(2):
         for d in order:
             red(0, half, d).start()
+
+    def pass_on(t):
+        gather(6, t).start()
+        gather(7, t + 4).start()
+
+    def relay(t):
+        gather(3, t).start()
+        gather(4, t).start()
+
+    loop(4, pass_on)
+    loop(8, relay)
     for half in range(2):
         total = summed(0, half)
         if half == 0:
@@ -297,12 +315,14 @@
             DMA((4,)),
         ],
         compiler_params=pltpu.CompilerParams(
-            collective_id=0, has_side_effects=True, vmem_limit_bytes=40 * 2**20
+            collective_id=0, has_side_effects=True, vmem_limit_bytes=67043328
         ),
         name="filter",
     )(hamiltonian, orbitals, adjacency)
 
 
+SIZE = 64
+EARLY = False
 TN = (((0,), (0,)), ((), ()))
 NN = (((1,), (0,)), ((), ()))
 
@@ -316,19 +336,20 @@
 
 
 def factor_block(tiles):
-    sub = lax.broadcasted_iota(jnp.int32, (8, 128), 0)
+    n, width = len(tiles), tiles[0].shape[1]
+    sub = lax.broadcasted_iota(jnp.int32, (8, width), 0)
     tiles = list(tiles)
     done = []
-    for s in range(8):
+    for s in range(n):
         tile = tiles[s]
         at = [[spread(tile, i, 8 * s + j) if j >= i else None for j in range(8)] for i in range(8)]
-        rows = [jnp.broadcast_to(tile[k:k + 1, :], (8, 128)) for k in range(8)]
+        rows = [jnp.broadcast_to(tile[k:k + 1, :], (8, width)) for k in range(8)]
         cols = {g: [jnp.broadcast_to(tiles[g][:, 8 * s + k:8 * s + k + 1], (8, 128)) for k in range(8)]
-                for g in range(s + 1, 8)}
+                for g in range(s + 1, n)}
+        wide = lambda x: jnp.concatenate([x] * (width // 128), axis=1)
         for k in range(8):
             r = lax.rsqrt(at[k][k])
-            r = r * (1.5 - 0.5 * at[k][k] * r * r)
-            rows[k] = rows[k] * r
+            rows[k] = rows[k] * wide(r)
             for j in range(k + 1, 8):
                 at[k][j] = at[k][j] * r
             for g in cols:
@@ -336,13 +357,13 @@
             for i in range(k + 1, 8):
                 for j in range(i, 8):
                     at[i][j] = at[i][j] - at[k][i] * at[k][j]
-                rows[i] = rows[i] - at[k][i] * rows[k]
+                rows[i] = rows[i] - wide(at[k][i]) * rows[k]
                 for g in cols:
                     cols[g][i] = cols[g][i] - at[k][i] * cols[g][k]
         for g in cols:
             t = tiles[g]
             for k in range(8):
-                t = t - cols[g][k] * rows[k]
+                t = t - wide(cols[g][k]) * rows[k]
             tiles[g] = t
         out = rows[0]
         for k in range(1, 8):
@@ -351,13 +372,26 @@
     return jnp.concatenate(done, axis=0)
 
 
-def finish_kernel(gram_a_ref, gram_b_ref, filt_hbm, low_hbm, basis_ref, factor_ref, work, rest, inv, filt, low, sem):
+def finish_kernel(
+    gram_a_hbm, gram_b_hbm, filt_hbm, low_hbm, basis_ref, factor_ref,
+    work, rest, inv, gram_a_ref, gram_b_ref, filt, low, sem,
+):
+    load_a = pltpu.make_async_copy(gram_a_hbm, gram_a_ref, sem.at[2])
+    load_a.start()
+    load_b = pltpu.make_async_copy(gram_b_hbm, gram_b_ref, sem.at[3])
+    load_b.start()
     load_f = pltpu.make_async_copy(filt_hbm, filt, sem.at[0])
     load_f.start()
     load_l = pltpu.make_async_copy(low_hbm, low, sem.at[1])
     load_l.start()
+    rest[...] = jnp.zeros_like(rest)
+    inv[...] = jnp.zeros_like(inv)
+    factor_ref[...] = jnp.zeros_like(factor_ref)
+    load_a.wait()
+    load_b.wait()
+
     def place(i, j, block):
-        if i // 2 > j // 2:
+        if 32 * i // SIZE > 32 * j // SIZE:
             i, j, block = j, i, block.T
         work[32 * i:32 * i + 32, 32 * j:32 * j + 32] = block
 
@@ -373,26 +407,43 @@
         place(o, left, top[:, 64:96])
         place(right, pair, top[:, 96:])
         place(right, left, jnp.concatenate([fold[:, 32 * q:32 * q + 32] for q in range(4)], axis=0))
-    eye = (lax.broadcasted_iota(jnp.int32, (64, 64), 0) == lax.broadcasted_iota(jnp.int32, (64, 64), 1)).astype(F32)
-    upper = lax.broadcasted_iota(jnp.int32, (64, 64), 0) <= lax.broadcasted_iota(jnp.int32, (64, 64), 1)
-    lower = lax.broadcasted_iota(jnp.int32, (64, 64), 0) >= lax.broadcasted_iota(jnp.int32, (64, 64), 1)
-    rest[...] = jnp.zeros_like(rest)
-    inv[...] = jnp.zeros_like(inv)
-    factor_ref[...] = jnp.zeros_like(factor_ref)
-    for p in range(4):
-        a, b = 64 * p, 64 * p + 64
-        block = jnp.concatenate([work[a:b, a:b], eye], axis=1)
-        solved = factor_block([block[8 * s:8 * s + 8] for s in range(8)])
-        factor_ref[a:b, a:b] = jnp.where(upper, solved[:, :64], 0.0)
-        own = jnp.where(lower, solved[:, 64:], 0.0)
-        inv[a:b, a:b] = own
-        if p > 0:
-            inv[a:b, :a] = exact_dot(own, rest[a:b, :a], NN)
-        if p < 3:
-            u = exact_dot(own, work[a:b, b:], NN)
-            factor_ref[a:b, b:] = u
-            work[b:, b:] = work[b:, b:] - exact_dot(u, u, TN)
-            rest[b:, :b] = rest[b:, :b] - exact_dot(u, inv[a:b, :b], TN)
+    eye = (lax.broadcasted_iota(jnp.int32, (SIZE, SIZE), 0) == lax.broadcasted_iota(jnp.int32, (SIZE, SIZE), 1)).astype(F32)
+    upper = lax.broadcasted_iota(jnp.int32, (SIZE, SIZE), 0) <= lax.broadcasted_iota(jnp.int32, (SIZE, SIZE), 1)
+    lower = lax.broadcasted_iota(jnp.int32, (SIZE, SIZE), 0) >= lax.broadcasted_iota(jnp.int32, (SIZE, SIZE), 1)
+    block = work[:SIZE, :SIZE]
+    later = None
+    for p in range(256 // SIZE):
+        a, b = SIZE * p, SIZE * p + SIZE
+        if EARLY and later:
+            later()
+        block = jnp.concatenate([block, eye], axis=1)
+        solved = factor_block([block[8 * s:8 * s + 8] for s in range(SIZE // 8)])
+        if later and not EARLY:
+            later()
+        own = jnp.where(lower, solved[:, SIZE:], 0.0)
+        if b < 256:
+            c = b + SIZE
+            u = exact_dot(own, work[a:b, b:c], NN)
+            block = work[b:c, b:c] - exact_dot(u, u, TN)
+
+        def later(a=a, b=b, own=own, solved=solved, u=u):
+            factor_ref[a:b, a:b] = jnp.where(upper, solved[:, :SIZE], 0.0)
+            inv[a:b, a:b] = own
+            if a > 0:
+                inv[a:b, :a] = exact_dot(own, rest[a:b, :a], NN)
+            if b < 256:
+                c = b + SIZE
+                factor_ref[a:b, b:c] = u
+                whole = u
+                if c < 256:
+                    v = exact_dot(own, work[a:b, c:], NN)
+                    factor_ref[a:b, c:] = v
+                    whole = jnp.concatenate([u, v], axis=1)
+                    work[b:c, c:] = work[b:c, c:] - exact_dot(u, v, TN)
+                    work[c:, c:] = work[c:, c:] - exact_dot(v, v, TN)
+                rest[b:, :b] = rest[b:, :b] - exact_dot(whole, inv[a:b, :b], TN)
+
+    later()
     orb = lax.axis_index("orb")
     mine = inv[pl.ds(pl.multiple_of(orb * 32, 32), 32), :]
     high = mine.astype(BF16)
@@ -411,18 +462,19 @@
 
 
 def finish_call(gram_a, gram_b, filt, low):
-    anywhere = pl.BlockSpec(memory_space=pl.ANY)
+    outside = pl.BlockSpec(memory_space=pltpu.HBM)
     vmem = pl.BlockSpec(memory_space=pltpu.VMEM)
     return pl.pallas_call(
         finish_kernel,
         out_shape=(jax.ShapeDtypeStruct((32, 2048), F32), jax.ShapeDtypeStruct((256, 256), F32)),
-        in_specs=[vmem, vmem, anywhere, anywhere],
+        in_specs=[outside] * 4,
         out_specs=(vmem, vmem),
         scratch_shapes=[
-            pltpu.VMEM((256, 256), F32), pltpu.VMEM((256, 256), F32), pltpu.VMEM((256, 256), F32),
-            pltpu.VMEM((8, 8, 32, 256), BF16), pltpu.VMEM((8, 32, 256), BF16), DMA((2,)),
+            *[pltpu.VMEM((256, 256), F32)] * 3,
+            pltpu.VMEM((8, 24, 128), F32), pltpu.VMEM((8, 16, 128), F32),
+            pltpu.VMEM((8, 8, 32, 256), BF16), pltpu.VMEM((8, 32, 256), BF16), DMA((4,)),
         ],
-        compiler_params=pltpu.CompilerParams(vmem_limit_bytes=40 * 2**20),
+        compiler_params=pltpu.CompilerParams(vmem_limit_bytes=67043328),
         name="finish",
     )(gram_a, gram_b, filt, low)
 

time: 72 us -> 66.8 us (0.928)
  local copies, waits for them, and re-layouts: 4.67 us -> 0 us
    unnamed x6 -> x0, local copies, waits for them, and re-layouts: 4.67 us -> none
    pallas_call x1, Pallas kernels: 13.3 us -> 12.4 us  [finish_call(): pl.pallas_call(finish_kernel, out_shape=(jax.ShapeDtypeStruct((32, 2048),...]
where the time goes in v3:
time: 66.8 us; the launch traced here: 66.6 us
  Pallas kernels  66 us (99%)
    pallas_call x1, Pallas kernels, filter_call(): pl.pallas_call(filter_kernel, out_shape=(jax.ShapeDtypeStruct((8, 24, 128...  53.6 us
    pallas_call x1, Pallas kernels, finish_call(): pl.pallas_call(finish_kernel, out_shape=(jax.ShapeDtypeStruct((32, 2048),...  12.4 us

profile of v3, /device:TPU:1, one launch (start us, length us, event | category | flops | bytes accessed | tf_op | source)
XLA Modules:
  0.0 66.6 jit_solution(5337528431941248467)
XLA Ops:
  0.6 53.6 %filter.1 = (f32[8,24,128]{2,1,0:T(8,128)}, f32[8,16,128]{2,1,0:T(8,128)}, bf16[8,8,32,256]{3,2,1,0:T(8,128)(2,1)}, bf16[8,32,256]{2,1,0:T(8,128)(2,1)}) custom-call(bf16[8,7,256,256]{3,2,1,0:T(8,128)(2,1)} %ham_hbm.1, bf16[32,2048]{1,0:T(8,128)(2,1)} %orb_hbm.1, s32[8,6]{1,0:T(8,128)} %adj_hbm.1), custom_call_target="tpu_custom_call" | custom-call | tf_op jit(solution)/shard_map/filter/pallas_call | solution.py:289
  54.2 12.4 %finish.1 = (f32[32,2048]{1,0:T(8,128)}, f32[256,256]{1,0:T(8,128)}) custom-call(f32[8,24,128]{2,1,0:T(8,128)} %get-tuple-element.6.gram_a_hbm, f32[8,16,128]{2,1,0:T(8,128)} %get-tuple-element.7.gram_b_hbm, bf16[8,8,32,256]{3,2,1,0:T(8,128)(2,1)} %get-tuple-element.8.filt_hbm, bf16[8,32,256]{2,1,0:T(8,128)(2,1)} %get-tuple-element.9.low_hbm), custom_call_target="tpu_custom_call" | custom-call | tf_op jit(solution)/shard_map/finish/pallas_call | solution.py:467

commit v4 on v3

--- a/solution.py
+++ b/solution.py
@@ -335,6 +335,10 @@
     return jnp.broadcast_to(x[i:i + 1, j:j + 1], (8, 128))
 
 
+def lane_spread(x, j):
+    return jnp.take_along_axis(x[:, :128], jnp.full((8, 128), j, jnp.int32), axis=1)
+
+
 def factor_block(tiles):
     n, width = len(tiles), tiles[0].shape[1]
     sub = lax.broadcasted_iota(jnp.int32, (8, width), 0)
@@ -342,9 +346,10 @@
     done = []
     for s in range(n):
         tile = tiles[s]
-        at = [[spread(tile, i, 8 * s + j) if j >= i else None for j in range(8)] for i in range(8)]
+        own = [lane_spread(tile, 8 * s + j) for j in range(8)]
+        at = [[jnp.broadcast_to(own[j][i:i + 1, :], (8, 128)) if j >= i else None for j in range(8)] for i in range(8)]
         rows = [jnp.broadcast_to(tile[k:k + 1, :], (8, width)) for k in range(8)]
-        cols = {g: [jnp.broadcast_to(tiles[g][:, 8 * s + k:8 * s + k + 1], (8, 128)) for k in range(8)]
+        cols = {g: [lane_spread(tiles[g], 8 * s + k) for k in range(8)]
                 for g in range(s + 1, n)}
         wide = lambda x: jnp.concatenate([x] * (width // 128), axis=1)
         for k in range(8):

time: 66.8 us -> 65.1 us (0.975)
  Pallas kernels: 66 us -> 64.3 us
    pallas_call x1, Pallas kernels: 12.4 us -> 10.8 us  [finish_call(): pl.pallas_call(finish_kernel, out_shape=(jax.ShapeDtypeStruct((32, 2048),...]
where the time goes in v4:
time: 65.1 us; the launch traced here: 65 us
  Pallas kernels  64.3 us (99%)
    pallas_call x1, Pallas kernels, filter_call(): pl.pallas_call(filter_kernel, out_shape=(jax.ShapeDtypeStruct((8, 24, 128...  53.6 us
    pallas_call x1, Pallas kernels, finish_call(): pl.pallas_call(finish_kernel, out_shape=(jax.ShapeDtypeStruct((32, 2048),...  10.8 us

profile of v4, /device:TPU:1, one launch (start us, length us, event | category | flops | bytes accessed | tf_op | source)
XLA Modules:
  0.0 65.0 jit_solution(1148342411135720099)
XLA Ops:
  0.6 53.6 %filter.1 = (f32[8,24,128]{2,1,0:T(8,128)}, f32[8,16,128]{2,1,0:T(8,128)}, bf16[8,8,32,256]{3,2,1,0:T(8,128)(2,1)}, bf16[8,32,256]{2,1,0:T(8,128)(2,1)}) custom-call(bf16[8,7,256,256]{3,2,1,0:T(8,128)(2,1)} %ham_hbm.1, bf16[32,2048]{1,0:T(8,128)(2,1)} %orb_hbm.1, s32[8,6]{1,0:T(8,128)} %adj_hbm.1), custom_call_target="tpu_custom_call" | custom-call | tf_op jit(solution)/shard_map/filter/pallas_call | solution.py:289
  54.2 10.8 %finish.1 = (f32[32,2048]{1,0:T(8,128)}, f32[256,256]{1,0:T(8,128)}) custom-call(f32[8,24,128]{2,1,0:T(8,128)} %get-tuple-element.6.gram_a_hbm, f32[8,16,128]{2,1,0:T(8,128)} %get-tuple-element.7.gram_b_hbm, bf16[8,8,32,256]{3,2,1,0:T(8,128)(2,1)} %get-tuple-element.8.filt_hbm, bf16[8,32,256]{2,1,0:T(8,128)(2,1)} %get-tuple-element.9.low_hbm), custom_call_target="tpu_custom_call" | custom-call | tf_op jit(solution)/shard_map/finish/pallas_call | solution.py:472

commit v5 on v4

--- a/solution.py
+++ b/solution.py
@@ -269,13 +269,12 @@
         for half in range(2):
             for d in order:
                 red(stage, half, d).wait_send()
-    for half in range(2):
+    out_a = pltpu.make_async_copy(gram_a, gram_a_out, out_sem.at[2])
+    out_b = pltpu.make_async_copy(gram_b, gram_b_out, out_sem.at[3])
+    for half, out in enumerate((out_a, out_b)):
         for d in order:
             share(half, d).wait_recv()
-    out_a = pltpu.make_async_copy(gram_a, gram_a_out, out_sem.at[2])
-    out_a.start()
-    out_b = pltpu.make_async_copy(gram_b, gram_b_out, out_sem.at[3])
-    out_b.start()
+        out.start()
     for half in range(2):
         for d in order:
             share(half, d).wait_send()
@@ -378,8 +377,8 @@
 
 
 def finish_kernel(
-    gram_a_hbm, gram_b_hbm, filt_hbm, low_hbm, basis_ref, factor_ref,
-    work, rest, inv, gram_a_ref, gram_b_ref, filt, low, sem,
+    gram_a_hbm, gram_b_hbm, filt_hbm, low_hbm, basis_hbm, factor_hbm,
+    basis_ref, factor_ref, work, rest, inv, gram_a_ref, gram_b_ref, filt, low, sem,
 ):
     load_a = pltpu.make_async_copy(gram_a_hbm, gram_a_ref, sem.at[2])
     load_a.start()
@@ -449,6 +448,8 @@
                 rest[b:, :b] = rest[b:, :b] - exact_dot(whole, inv[a:b, :b], TN)
 
     later()
+    store_f = pltpu.make_async_copy(factor_ref, factor_hbm, sem.at[4])
+    store_f.start()
     orb = lax.axis_index("orb")
     mine = inv[pl.ds(pl.multiple_of(orb * 32, 32), 32), :]
     high = mine.astype(BF16)
@@ -460,24 +461,30 @@
     load_f.wait()
     load_l.wait()
 
+    stores = [store_f]
     for e in range(8):
         d = lax.dot_general(stack, filt[e].reshape(256, 256), NN, preferred_element_type=F32)
         c = lax.dot_general(here, low[e], NN, preferred_element_type=F32)
         basis_ref[:, e * 256:(e + 1) * 256] = d[:32] + (d[32:64] + (d[64:] + c))
+        if e % 2:
+            part = pl.ds(e * 256 - 256, 512)
+            stores.append(pltpu.make_async_copy(basis_ref.at[:, part], basis_hbm.at[:, part], sem.at[5 + e // 2]))
+            stores[-1].start()
+    for store in stores:
+        store.wait()
 
 
 def finish_call(gram_a, gram_b, filt, low):
     outside = pl.BlockSpec(memory_space=pltpu.HBM)
-    vmem = pl.BlockSpec(memory_space=pltpu.VMEM)
     return pl.pallas_call(
         finish_kernel,
         out_shape=(jax.ShapeDtypeStruct((32, 2048), F32), jax.ShapeDtypeStruct((256, 256), F32)),
         in_specs=[outside] * 4,
-        out_specs=(vmem, vmem),
+        out_specs=(outside, outside),
         scratch_shapes=[
-            *[pltpu.VMEM((256, 256), F32)] * 3,
+            pltpu.VMEM((32, 2048), F32), *[pltpu.VMEM((256, 256), F32)] * 4,
             pltpu.VMEM((8, 24, 128), F32), pltpu.VMEM((8, 16, 128), F32),
-            pltpu.VMEM((8, 8, 32, 256), BF16), pltpu.VMEM((8, 32, 256), BF16), DMA((4,)),
+            pltpu.VMEM((8, 8, 32, 256), BF16), pltpu.VMEM((8, 32, 256), BF16), DMA((9,)),
         ],
         compiler_params=pltpu.CompilerParams(vmem_limit_bytes=67043328),
         name="finish",

time: 65.1 us -> 65 us (level)
  no operation moved by 1% of the time
where the time goes in v5:
time: 65 us; the launch traced here: 64.9 us
  Pallas kernels  64.3 us (99%)
    pallas_call x1, Pallas kernels, filter_call(): pl.pallas_call(filter_kernel, out_shape=(jax.ShapeDtypeStruct((8, 24, 128...  53.5 us
    pallas_call x1, Pallas kernels, finish_call(): pl.pallas_call(finish_kernel, out_shape=(jax.ShapeDtypeStruct((32, 2048),...  10.7 us

profile of v5, /device:TPU:1, one launch (start us, length us, event | category | flops | bytes accessed | tf_op | source)
XLA Modules:
  0.0 64.9 jit_solution(6481212199801480841)
XLA Ops:
  0.6 53.5 %filter.1 = (f32[8,24,128]{2,1,0:T(8,128)}, f32[8,16,128]{2,1,0:T(8,128)}, bf16[8,8,32,256]{3,2,1,0:T(8,128)(2,1)}, bf16[8,32,256]{2,1,0:T(8,128)(2,1)}) custom-call(bf16[8,7,256,256]{3,2,1,0:T(8,128)(2,1)} %ham_hbm.1, bf16[32,2048]{1,0:T(8,128)(2,1)} %orb_hbm.1, s32[8,6]{1,0:T(8,128)} %adj_hbm.1), custom_call_target="tpu_custom_call" | custom-call | tf_op jit(solution)/shard_map/filter/pallas_call | solution.py:288
  54.2 10.7 %finish.1 = (f32[32,2048]{1,0:T(8,128)}, f32[256,256]{1,0:T(8,128)}) custom-call(f32[8,24,128]{2,1,0:T(8,128)} %get-tuple-element.6.gram_a_hbm, f32[8,16,128]{2,1,0:T(8,128)} %get-tuple-element.7.gram_b_hbm, bf16[8,8,32,256]{3,2,1,0:T(8,128)(2,1)} %get-tuple-element.8.filt_hbm, bf16[8,32,256]{2,1,0:T(8,128)(2,1)} %get-tuple-element.9.low_hbm), custom_call_target="tpu_custom_call" | custom-call | tf_op jit(solution)/shard_map/finish/pallas_call | solution.py:479
